TPU v7x, 512 devices: a whole 4x4x16 slice. The times are simulated.
512 devices in a mesh: freq: 64 (over z, x_hi, core), space: 8 (over x_lo, y).
Axes of the slice: x: 4 (x_hi: 2, x_lo: 2; x = x_hi * 2 + x_lo), y: 4, z: 16, core: 2. Of those that a mesh axis runs over, the one named last changes fastest.
Arguments:
- series: bfloat16 [2048, 131072], P('freq', 'space')
- starts: int32 [7], replicated, may hold values from 0 to 1536, as said below
- freqs: int32 [64], replicated, may hold values from 0 to 511, as said below
- alpha: int32 [1], replicated, may hold values from 1 to 63
Outputs:
- spectra: bfloat16 [64, 2, 7, 131072], P('freq', None, None, 'space')
- gram: float32 [64, 2, 63, 63], P('freq')
Inputs may be any that keep to these rules, and one draw needn't show every extreme that they name: `starts`: increasing; the first is 0, the last 1536; consecutive ones lie 512 / 4 to 384 apart. `freqs`: 64 distinct bins, 0 and 511 among them.
All inputs are finite; a program needn't handle non-finite values.
Results may differ from a plain program's by a relative error of at most 0.005.
Values may be sent and summed in bfloat16 or wider, within the bound.
No kernel may reach another device: no remote copies, remote signals or barrier semaphores. Data moves between devices by JAX's collectives and lax.ppermute only.
A program may use at most 64 MiB of HBM per device.

v0:
```python
import math
import jax
import jax.numpy as jnp
from jax import lax
from jax.sharding import PartitionSpec as P

NFFT = 512
NBLK = 7
HALF = 4
SHIFTS = 9
ORDER = SHIFTS * NBLK
ENTRIES = 2 * ORDER * ORDER


def transform_table(freqs, alpha):
    sample_index = jnp.arange(NFFT, dtype=jnp.int32)
    shift_index = jnp.arange(SHIFTS, dtype=jnp.int32) - HALF
    freq_bins = jnp.mod(freqs[:, None] + shift_index[None, :] * alpha[0], NFFT)
    phase_steps = jnp.mod(freq_bins[:, :, None] * sample_index[None, None, :], NFFT)
    phase = phase_steps.astype(jnp.float32) * (2.0 * math.pi / NFFT)
    sample_float = sample_index.astype(jnp.float32)
    window_shape = 0.5 - 0.5 * jnp.cos(sample_float * (2.0 * math.pi / NFFT))
    window_scale = window_shape / jnp.sqrt(jnp.sum(window_shape * window_shape))
    real_part = window_scale * jnp.cos(phase)
    imag_part = -(window_scale * jnp.sin(phase))
    return jnp.stack([real_part, imag_part], axis=1).astype(jnp.bfloat16)


def split_quadrants(products, order):
    real_gram = products[..., :order, :order] + products[..., order:, order:]
    imag_gram = products[..., :order, order:] - products[..., order:, :order]
    return jnp.stack([real_gram, imag_gram], axis=-3)


def per_device(series, starts, freqs, alpha):
    slab_cells = series.shape[1]
    n_space = lax.axis_size("space")
    n_freq = freqs.shape[0]
    total_cells = slab_cells * n_space
    cells = slab_cells // n_freq
    piece = -(-ENTRIES // (n_space * 128)) * 128
    rows = lax.all_to_all(series, "freq", split_axis=1, concat_axis=0, tiled=True)
    flat_table = transform_table(freqs, alpha).reshape(n_freq * 2 * SHIFTS, NFFT)
    blocks = []
    for block in range(NBLK):
        block_rows = lax.dynamic_slice_in_dim(rows, starts[block], NFFT, 0)
        spec_block = jnp.dot(flat_table, block_rows, preferred_element_type=jnp.float32)
        blocks.append(spec_block.astype(jnp.bfloat16).reshape(n_freq, 2, SHIFTS, cells))
    blockspec = jnp.stack(blocks, axis=3)
    stacked = blockspec.reshape(n_freq, 2 * ORDER, cells)
    products = jnp.einsum("jrc,jsc->jrs", stacked, stacked, preferred_element_type=jnp.float32)
    partial = split_quadrants(products, ORDER).reshape(n_freq, ENTRIES).astype(jnp.bfloat16)
    partial = jnp.pad(partial, ((0, 0), (0, n_space * piece - ENTRIES)))
    partial = jnp.transpose(partial.reshape(n_freq, n_space, piece), (1, 0, 2))
    gathered = lax.all_to_all(partial, "space", split_axis=0, concat_axis=0, tiled=True)
    slab_sum = jnp.sum(gathered.astype(jnp.float32), axis=0).astype(jnp.bfloat16)
    own = blockspec[:, :, HALF].reshape(n_freq, 2 * NBLK * cells)
    packed = jnp.concatenate([own, slab_sum], axis=1)
    packed = packed.reshape(n_freq, packed.shape[1] // 128, 128)
    received = lax.all_to_all(packed, "freq", split_axis=0, concat_axis=0, tiled=True)
    received = received.reshape(n_freq, -1)
    own = received[:, : 2 * NBLK * cells].reshape(n_freq, 2, NBLK, cells)
    spectra = jnp.transpose(own, (1, 2, 0, 3)).reshape(1, 2, NBLK, slab_cells)
    gram_piece = jnp.sum(received[:, 2 * NBLK * cells :].astype(jnp.float32), axis=0)
    spread = jnp.broadcast_to(
        gram_piece.reshape(1, piece // 128, 128), (n_space, piece // 128, 128)
    )
    pieces = lax.all_to_all(spread, "space", split_axis=0, concat_axis=0, tiled=True)
    gram = pieces.reshape(-1)[:ENTRIES].reshape(1, 2, ORDER, ORDER) / total_cells
    return (spectra, gram)


def solution(mesh):
    placed = (P("freq", "space"), P(), P(), P())
    return jax.shard_map(
        per_device,
        mesh=mesh,
        in_specs=placed,
        out_specs=(P("freq", None, None, "space"), P("freq", None, None, None)),
        check_vma=False,
    )
```

profile of v0, /device:TPU:4, one launch (start us, length us, event | category | flops | bytes accessed | tf_op | source)
XLA Modules:
  0.0 204.1 jit_solution(17525329280515386806)
XLA Ops:
  0.6 2.3 %copy.49 = bf16[4,64,8,256]{3,2,0,1:T(8,128)(2,1)} copy(bf16[4,64,8,256]{3,2,1,0:T(8,128)(2,1)} %bitcast.54) | data formatting | bytes 2097152 | tf_op jit(solution)/shard_map/all_to_all | solution.py:42
  3.0 18.9 %all-to-all-start = ((bf16[32,64,256]{2,0,1:T(8,128)(2,1)}), bf16[32,64,256]{2,0,1:T(8,128)(2,1)}, u32[]{:S(2)}, u32[]{:S(2)}) async-start(bf16[32,64,256]{2,0,1:T(8,128)(2,1)} %bitcast.45), calls=%async_computation | async-start | bytes 2097152 | tf_op jit(solution)/shard_map/all_to_all | solution.py:42
  33.3 5.4 %multiply_convert_fusion = (bf16[64,1,9,512]{3,0,2,1:T(8,128)(2,1)S(1)}, bf16[64,1,9,512]{3,0,2,1:T(8,128)(2,1)S(1)}) fusion(s32[64,9]{0,1:T(8,128)S(1)} %add_select_fusion.2, f32[512]{0:T(512)S(1)} %fusion.20), kind=kLoop, calls=%fused_computation.22 | loop fusion | flops 5603328 | bytes 1184000 | tf_op jit(solution)/shard_map/convert.5
  44.5 33.4 %all-to-all-done = bf16[32,64,256]{2,0,1:T(8,128)(2,1)} async-done(((bf16[32,64,256]{2,0,1:T(8,128)(2,1)}), bf16[32,64,256]{2,0,1:T(8,128)(2,1)}, u32[]{:S(2)}, u32[]{:S(2)}) %all-to-all-start) | async-done | bytes 1048608 | tf_op jit(solution)/shard_map/all_to_all | solution.py:42
  77.9 1.5 convolution_convert_fusion.6
  80.6 1.5 convolution_convert_fusion.5
  82.3 2.3 %convolution_convert_fusion.4 = bf16[1152,256]{1,0:T(8,128)(2,1)} fusion(bf16[1152,512]{1,0:T(8,128)(2,1)S(1)} %convert_element_type.62, bf16[2048,256]{1,0:T(8,128)(2,1)} %bitcast.2, s32[]{:T(128)S(6)} %select_n.53), kind=kOutput, calls=%fused_computation.6 | convolution fusion | flops 302284800 | bytes 2031620 | tf_op jit(solution)/shard_map/dot_general | solution.py:47
  86.0 2.3 %convolution_convert_fusion.3 = bf16[1152,256]{1,0:T(8,128)(2,1)} fusion(bf16[1152,512]{1,0:T(8,128)(2,1)S(1)} %convert_element_type.62, bf16[2048,256]{1,0:T(8,128)(2,1)} %bitcast.2, s32[]{:T(128)S(6)} %select_n.54), kind=kOutput, calls=%fused_computation.5 | convolution fusion | flops 302284800 | bytes 2031620 | tf_op jit(solution)/shard_map/dot_general | solution.py:47
  88.3 2.2 %stack_reshape.24 = bf16[64,2,9,1,256]{4,2,1,0,3:T(8,128)(2,1)} reshape(bf16[1152,256]{1,0:T(8,128)(2,1)} %convolution_convert_fusion.3) | data formatting | bytes 1179648 | tf_op jit(solution)/shard_map/stack;reshape | solution.py:49
  90.5 2.3 %convolution_convert_fusion.2 = bf16[1152,256]{1,0:T(8,128)(2,1)} fusion(bf16[1152,512]{1,0:T(8,128)(2,1)S(1)} %convert_element_type.62, bf16[2048,256]{1,0:T(8,128)(2,1)} %bitcast.2, s32[]{:T(128)S(6)} %select_n.55), kind=kOutput, calls=%fused_computation.4 | convolution fusion | flops 302284800 | bytes 2031620 | tf_op jit(solution)/shard_map/dot_general | solution.py:47
  92.8 2.1 %stack_reshape.25 = bf16[64,2,9,1,256]{4,2,1,0,3:T(8,128)(2,1)} reshape(bf16[1152,256]{1,0:T(8,128)(2,1)} %convolution_convert_fusion.2) | data formatting | bytes 1179648 | tf_op jit(solution)/shard_map/stack;reshape | solution.py:49
  94.9 2.3 %convolution_convert_fusion.1 = bf16[1152,256]{1,0:T(8,128)(2,1)} fusion(bf16[1152,512]{1,0:T(8,128)(2,1)S(1)} %convert_element_type.62, bf16[2048,256]{1,0:T(8,128)(2,1)} %bitcast.2, s32[]{:T(128)S(6)} %select_n.56), kind=kOutput, calls=%fused_computation.3 | convolution fusion | flops 302284800 | bytes 2031620 | tf_op jit(solution)/shard_map/dot_general | solution.py:47
  97.2 2.1 %stack_reshape.26 = bf16[64,2,9,1,256]{4,2,1,0,3:T(8,128)(2,1)} reshape(bf16[1152,256]{1,0:T(8,128)(2,1)} %convolution_convert_fusion.1) | data formatting | bytes 1179648 | tf_op jit(solution)/shard_map/stack;reshape | solution.py:49
  99.3 2.3 %convolution_convert_fusion = bf16[1152,256]{1,0:T(8,128)(2,1)} fusion(bf16[1152,512]{1,0:T(8,128)(2,1)S(1)} %convert_element_type.62, bf16[2048,256]{1,0:T(8,128)(2,1)} %bitcast.2, s32[]{:T(128)S(6)} %select_n.57), kind=kOutput, calls=%fused_computation.2 | convolution fusion | flops 302284800 | bytes 2031620 | tf_op jit(solution)/shard_map/dot_general | solution.py:47
  101.6 1.5 stack_reshape.27
  111.1 5.6 %copy.33 = bf16[64,2,9,7,256]{4,0,3,2,1:T(8,128)(2,1)S(1)} copy(bf16[64,2,9,7,256]{4,2,1,0,3:T(8,128)(2,1)} %constant_dynamic-update-slice_fusion) | data formatting | bytes 8257536 | tf_op jit(solution)/shard_map/stack | solution.py:49
  116.7 4.6 %fusion = f32[64,126,126]{2,1,0:T(8,128)S(1)} fusion(bf16[64,126,256]{2,0,1:T(8,128)(2,1)S(1)} %bitcast.48), kind=kOutput, calls=%fused_computation | convolution fusion | flops 520224768 | bytes 8193024 | tf_op jit(solution)/shard_map/jrc,jsc->jrs/dot_general | solution.py:51
  123.2 3.3 %convert_element_type.70 = bf16[64,7938]{1,0:T(8,128)(2,1)S(1)} reshape(bf16[64,2,63,63]{3,2,1,0:T(8,128)(2,1)S(1)} %copy.36) | data formatting | bytes 2032128 | tf_op jit(solution)/shard_map/convert_element_type | solution.py:52
  127.7 5.1 %all-to-all-start.1 = ((bf16[8,64,1024]{2,1,0:T(8,128)(2,1)}), bf16[8,64,1024]{2,1,0:T(8,128)(2,1)S(1)}, u32[]{:S(2)}, u32[]{:S(2)}) async-start(bf16[8,64,1024]{2,1,0:T(8,128)(2,1)} %bitcast.44), calls=%async_computation.1 | async-start | bytes 2097152 | tf_op jit(solution)/shard_map/all_to_all | solution.py:55
  132.8 3.0 %slice.60 = bf16[64,2,1,7,256]{4,2,1,0,3:T(2,128)(2,1)S(1)} slice(bf16[64,2,9,7,256]{4,2,1,0,3:T(8,128)(2,1)} %constant_dynamic-update-slice_fusion), slice={[0:64], [0:2], [4:5], [0:7], [0:256]} | slice | bytes 917504 | tf_op jit(solution)/shard_map/slice | solution.py:57
  136.8 9.9 %all-to-all-done.1 = bf16[8,64,1024]{2,1,0:T(8,128)(2,1)S(1)} async-done(((bf16[8,64,1024]{2,1,0:T(8,128)(2,1)}), bf16[8,64,1024]{2,1,0:T(8,128)(2,1)S(1)}, u32[]{:S(2)}, u32[]{:S(2)}) %all-to-all-start.1) | async-done | bytes 1048608 | tf_op jit(solution)/shard_map/all_to_all | solution.py:55
  147.3 45.3 %all_to_all.34 = bf16[64,36,128]{2,1,0:T(8,128)(2,1)S(1)} all-to-all(bf16[64,36,128]{2,1,0:T(8,128)(2,1)S(1)} %reshape.166), channel_id=1, replica_groups=mesh['freq'=64,'space'=8] {'freq'}, dimensions={0} | all-to-all | bytes 1179648 | tf_op jit(solution)/shard_map/all_to_all | solution.py:60
  193.3 3.6 %all-to-all-start.3 = ((f32[8,8,128]{2,1,0:T(8,128)}), f32[8,8,128]{2,1,0:T(8,128)S(1)}, u32[]{:S(2)}, u32[]{:S(2)}) async-start(f32[8,8,128]{2,1,0:T(8,128)} %broadcast_in_dim.5), calls=%async_computation.3 | async-start | bytes 65536 | tf_op jit(solution)/shard_map/all_to_all | solution.py:68
  198.6 4.6 %all-to-all-done.3 = f32[8,8,128]{2,1,0:T(8,128)S(1)} async-done(((f32[8,8,128]{2,1,0:T(8,128)}), f32[8,8,128]{2,1,0:T(8,128)S(1)}, u32[]{:S(2)}, u32[]{:S(2)}) %all-to-all-start.3) | async-done | bytes 32800 | tf_op jit(solution)/shard_map/all_to_all | solution.py:68
  (48 shorter events, 21.5 us)
Async XLA Ops:
  3.0 18.9 %copy-start.3 = (s32[7]{0:T(128)S(1)}, s32[7]{0:T(128)}, u32[]{:S(2)}) copy-start(s32[7]{0:T(128)} %param.5) | copy-start | bytes 88
  3.0 30.3 %copy-start.4 = (s32[64]{0:T(128)S(1)}, s32[64]{0:T(128)}, u32[]{:S(2)}) copy-start(s32[64]{0:T(128)} %param.6) | copy-start | bytes 772
  3.0 74.9 %all-to-all-start = ((bf16[32,64,256]{2,0,1:T(8,128)(2,1)}), bf16[32,64,256]{2,0,1:T(8,128)(2,1)}, u32[]{:S(2)}, u32[]{:S(2)}) async-start(bf16[32,64,256]{2,0,1:T(8,128)(2,1)} %bitcast.45), calls=%async_computation | async-start | bytes 2097152 | tf_op jit(solution)/shard_map/all_to_all | solution.py:42
  104.2 1.6 copy-start
  105.8 1.6 copy-start.1
  107.4 1.6 copy-start.2
  127.7 19.0 %all-to-all-start.1 = ((bf16[8,64,1024]{2,1,0:T(8,128)(2,1)}), bf16[8,64,1024]{2,1,0:T(8,128)(2,1)S(1)}, u32[]{:S(2)}, u32[]{:S(2)}) async-start(bf16[8,64,1024]{2,1,0:T(8,128)(2,1)} %bitcast.44), calls=%async_computation.1 | async-start | bytes 2097152 | tf_op jit(solution)/shard_map/all_to_all | solution.py:55
  193.3 9.9 %all-to-all-start.3 = ((f32[8,8,128]{2,1,0:T(8,128)}), f32[8,8,128]{2,1,0:T(8,128)S(1)}, u32[]{:S(2)}, u32[]{:S(2)}) async-start(f32[8,8,128]{2,1,0:T(8,128)} %broadcast_in_dim.5), calls=%async_computation.3 | async-start | bytes 65536 | tf_op jit(solution)/shard_map/all_to_all | solution.py:68
where the time goes:
time: 205 us; the launch traced here: 204 us
  waiting for transfers between devices  48 us (23%)
  blocking collectives  45.3 us (22%)
  local copies, waits for them, and re-layouts  40.9 us (20%)
  starting transfers between devices  27.7 us (14%)
  matrix products  19 us (9%)
  between operations  15.1 us (7%)
  other arithmetic  8.18 us (4%)
    all_to_all x1, blocking collectives, per_device(): lax.all_to_all(packed, 'freq', split_axis=0, concat_axis=0, tiled=True)  45.3 us
    all_to_all x1, waiting for transfers between devices, per_device(): lax.all_to_all(series, 'freq', split_axis=1, concat_axis=0, tiled=True)  33.4 us
    all_to_all x1, starting transfers between devices, per_device(): lax.all_to_all(series, 'freq', split_axis=1, concat_axis=0, tiled=True)  18.9 us
    another operation x9, local copies, waits for them, and re-layouts, per_device(): blockspec = jnp.stack(blocks, axis=3)  16.4 us
    dot_general x7, matrix products, per_device(): jnp.dot(flat_table, block_rows, preferred_element_type=jnp.float32)  14.3 us
    all_to_all x1, waiting for transfers between devices, per_device(): lax.all_to_all(partial, 'space', split_axis=0, concat_axis=0, tiled=True)  9.93 us
    unnamed x18, local copies, waits for them, and re-layouts  8.78 us
    another operation x1, other arithmetic  5.37 us
  transfers between devices with their start and end apart: 3, of which 3 were waited for; matrix products, arithmetic and copies ran while one was open for 7% of the time, Pallas kernels for 0%

commit v1 on v0

--- a/solution.py
+++ b/solution.py
@@ -39,7 +39,10 @@
     total_cells = slab_cells * n_space
     cells = slab_cells // n_freq
     piece = -(-ENTRIES // (n_space * 128)) * 128
-    rows = lax.all_to_all(series, "freq", split_axis=1, concat_axis=0, tiled=True)
+    rows = jnp.concatenate(
+        lax.all_to_all(jnp.stack(jnp.split(series, lax.axis_size("freq"), axis=1)), "freq", 0, 0),
+        axis=0,
+    )
     flat_table = transform_table(freqs, alpha).reshape(n_freq * 2 * SHIFTS, NFFT)
     blocks = []
     for block in range(NBLK):

time: 205 us -> 291 us (1.42); the launches traced: 204 us -> 286 us
  local copies, waits for them, and re-layouts: 40.9 us -> 123 us
    unnamed x18 -> x81, local copies, waits for them, and re-layouts: 8.78 us -> 91.8 us
  transfers between devices with their start and end apart: 3 -> 3, of which waited for: 3 -> 3; matrix products, arithmetic and copies ran while one was open for 7% -> 5% of each run, Pallas kernels for 0% -> 0%
where the time goes in v1:
time: 291 us; the launch traced here: 286 us
  local copies, waits for them, and re-layouts  123 us (42%)
  waiting for transfers between devices  48 us (16%)
  blocking collectives  45.3 us (16%)
  starting transfers between devices  27.5 us (9%)
  matrix products  18.9 us (6%)
  between operations  15.1 us (5%)
  other arithmetic  8.18 us (3%)
    unnamed x81, local copies, waits for them, and re-layouts  91.8 us
    all_to_all x1, blocking collectives, per_device(): lax.all_to_all(packed, 'freq', split_axis=0, concat_axis=0, tiled=True)  45.3 us
    all_to_all x1, waiting for transfers between devices, per_device(): lax.all_to_all(jnp.stack(jnp.split(series, lax.axis_size('freq'), axis=1)...  33.4 us
    all_to_all x1, starting transfers between devices, per_device(): lax.all_to_all(jnp.stack(jnp.split(series, lax.axis_size('freq'), axis=1)...  18.8 us
    another operation x9, local copies, waits for them, and re-layouts, per_device(): blockspec = jnp.stack(blocks, axis=3)  16.4 us
    dot_general x7, matrix products, per_device(): jnp.dot(flat_table, block_rows, preferred_element_type=jnp.float32)  14.3 us
    all_to_all x1, waiting for transfers between devices, per_device(): lax.all_to_all(partial, 'space', split_axis=0, concat_axis=0, tiled=True)  9.92 us
  transfers between devices with their start and end apart: 3, of which 3 were waited for; matrix products, arithmetic and copies ran while one was open for 5% of the time, Pallas kernels for 0%

profile of v1, /device:TPU:4, one launch (start us, length us, event | category | flops | bytes accessed | tf_op | source)
XLA Modules:
  0.0 286.0 jit_solution(7362460236017686288)
XLA Ops:
  74.4 1.3 constant_dynamic-update-slice_fusion.7
  85.0 18.8 %all-to-all-start = ((bf16[64,32,256]{2,1,0:T(8,128)(2,1)}), bf16[64,32,256]{2,1,0:T(8,128)(2,1)}, u32[]{:S(2)}, u32[]{:S(2)}) async-start(bf16[64,32,256]{2,1,0:T(8,128)(2,1)} %constant_dynamic-update-slice_fusion), calls=%async_computation | async-start | bytes 2097152 | tf_op jit(solution)/shard_map/all_to_all | solution.py:43
  115.2 5.4 %multiply_convert_fusion = (bf16[64,1,9,512]{3,0,2,1:T(8,128)(2,1)S(1)}, bf16[64,1,9,512]{3,0,2,1:T(8,128)(2,1)S(1)}) fusion(s32[64,9]{0,1:T(8,128)S(1)} %add_select_fusion.2, f32[512]{0:T(512)S(1)} %fusion.20), kind=kLoop, calls=%fused_computation.22 | loop fusion | flops 5603328 | bytes 1184000 | tf_op jit(solution)/shard_map/convert.5
  126.3 33.4 %all-to-all-done = bf16[64,32,256]{2,1,0:T(8,128)(2,1)} async-done(((bf16[64,32,256]{2,1,0:T(8,128)(2,1)}), bf16[64,32,256]{2,1,0:T(8,128)(2,1)}, u32[]{:S(2)}, u32[]{:S(2)}) %all-to-all-start) | async-done | bytes 1048608 | tf_op jit(solution)/shard_map/all_to_all | solution.py:43
  159.8 1.4 convolution_convert_fusion.6
  162.5 1.4 convolution_convert_fusion.5
  164.2 2.3 convolution_convert_fusion.4
  167.8 2.3 convolution_convert_fusion.3
  170.1 2.2 stack_reshape.24
  172.3 2.3 convolution_convert_fusion.2
  174.6 2.1 stack_reshape.25
  176.7 2.3 convolution_convert_fusion.1
  179.0 2.1 stack_reshape.26
  181.2 2.3 convolution_convert_fusion
  183.4 1.5 stack_reshape.27
  192.9 5.6 %copy.30 = bf16[64,2,9,7,256]{4,0,3,2,1:T(8,128)(2,1)S(1)} copy(bf16[64,2,9,7,256]{4,2,1,0,3:T(8,128)(2,1)} %constant_dynamic-update-slice_fusion.64) | data formatting | bytes 8257536 | tf_op jit(solution)/shard_map/stack | solution.py:52
  198.6 4.6 %fusion = f32[64,126,126]{2,1,0:T(8,128)S(1)} fusion(bf16[64,126,256]{2,0,1:T(8,128)(2,1)S(1)} %bitcast.170), kind=kOutput, calls=%fused_computation | convolution fusion | flops 520224768 | bytes 8193024 | tf_op jit(solution)/shard_map/jrc,jsc->jrs/dot_general | solution.py:54
  205.1 3.3 %convert_element_type.70 = bf16[64,7938]{1,0:T(8,128)(2,1)S(1)} reshape(bf16[64,2,63,63]{3,2,1,0:T(8,128)(2,1)S(1)} %copy.33) | data formatting | bytes 2032128 | tf_op jit(solution)/shard_map/convert_element_type | solution.py:55
  209.5 5.1 %all-to-all-start.1 = ((bf16[8,64,1024]{2,1,0:T(8,128)(2,1)}), bf16[8,64,1024]{2,1,0:T(8,128)(2,1)S(1)}, u32[]{:S(2)}, u32[]{:S(2)}) async-start(bf16[8,64,1024]{2,1,0:T(8,128)(2,1)} %bitcast.167), calls=%async_computation.1 | async-start | bytes 2097152 | tf_op jit(solution)/shard_map/all_to_all | solution.py:58
  214.6 3.0 %slice.60 = bf16[64,2,1,7,256]{4,2,1,0,3:T(2,128)(2,1)S(1)} slice(bf16[64,2,9,7,256]{4,2,1,0,3:T(8,128)(2,1)} %constant_dynamic-update-slice_fusion.64), slice={[0:64], [0:2], [4:5], [0:7], [0:256]} | slice | bytes 917504 | tf_op jit(solution)/shard_map/slice | solution.py:60
  218.6 9.9 %all-to-all-done.1 = bf16[8,64,1024]{2,1,0:T(8,128)(2,1)S(1)} async-done(((bf16[8,64,1024]{2,1,0:T(8,128)(2,1)}), bf16[8,64,1024]{2,1,0:T(8,128)(2,1)S(1)}, u32[]{:S(2)}, u32[]{:S(2)}) %all-to-all-start.1) | async-done | bytes 1048608 | tf_op jit(solution)/shard_map/all_to_all | solution.py:58
  229.1 45.3 %all_to_all.20 = bf16[64,36,128]{2,1,0:T(8,128)(2,1)S(1)} all-to-all(bf16[64,36,128]{2,1,0:T(8,128)(2,1)S(1)} %reshape.167), channel_id=1, replica_groups=mesh['freq'=64,'space'=8] {'freq'}, dimensions={0} | all-to-all | bytes 1179648 | tf_op jit(solution)/shard_map/all_to_all | solution.py:63
  275.2 3.6 %all-to-all-start.3 = ((f32[8,8,128]{2,1,0:T(8,128)}), f32[8,8,128]{2,1,0:T(8,128)S(1)}, u32[]{:S(2)}, u32[]{:S(2)}) async-start(f32[8,8,128]{2,1,0:T(8,128)} %broadcast_in_dim.5), calls=%async_computation.3 | async-start | bytes 65536 | tf_op jit(solution)/shard_map/all_to_all | solution.py:71
  280.4 4.6 %all-to-all-done.3 = f32[8,8,128]{2,1,0:T(8,128)S(1)} async-done(((f32[8,8,128]{2,1,0:T(8,128)}), f32[8,8,128]{2,1,0:T(8,128)S(1)}, u32[]{:S(2)}, u32[]{:S(2)}) %all-to-all-start.3) | async-done | bytes 32800 | tf_op jit(solution)/shard_map/all_to_all | solution.py:71
  (111 shorter events, 104.4 us)
Async XLA Ops:
  74.4 29.4 %copy-start.3 = (s32[7]{0:T(128)S(1)}, s32[7]{0:T(128)}, u32[]{:S(2)}) copy-start(s32[7]{0:T(128)} %param.5) | copy-start | bytes 88
  77.0 38.1 %copy-start.4 = (s32[64]{0:T(128)S(1)}, s32[64]{0:T(128)}, u32[]{:S(2)}) copy-start(s32[64]{0:T(128)} %param.6) | copy-start | bytes 772
  85.0 74.8 %all-to-all-start = ((bf16[64,32,256]{2,1,0:T(8,128)(2,1)}), bf16[64,32,256]{2,1,0:T(8,128)(2,1)}, u32[]{:S(2)}, u32[]{:S(2)}) async-start(bf16[64,32,256]{2,1,0:T(8,128)(2,1)} %constant_dynamic-update-slice_fusion), calls=%async_computation | async-start | bytes 2097152 | tf_op jit(solution)/shard_map/all_to_all | solution.py:43
  186.0 1.6 copy-start
  187.6 1.6 copy-start.1
  189.2 1.6 copy-start.2
  209.5 19.0 %all-to-all-start.1 = ((bf16[8,64,1024]{2,1,0:T(8,128)(2,1)}), bf16[8,64,1024]{2,1,0:T(8,128)(2,1)S(1)}, u32[]{:S(2)}, u32[]{:S(2)}) async-start(bf16[8,64,1024]{2,1,0:T(8,128)(2,1)} %bitcast.167), calls=%async_computation.1 | async-start | bytes 2097152 | tf_op jit(solution)/shard_map/all_to_all | solution.py:58
  275.2 9.9 %all-to-all-start.3 = ((f32[8,8,128]{2,1,0:T(8,128)}), f32[8,8,128]{2,1,0:T(8,128)S(1)}, u32[]{:S(2)}, u32[]{:S(2)}) async-start(f32[8,8,128]{2,1,0:T(8,128)} %broadcast_in_dim.5), calls=%async_computation.3 | async-start | bytes 65536 | tf_op jit(solution)/shard_map/all_to_all | solution.py:71
